TPU v7x, 32 devices: a whole 2x2x4 slice. The times are simulated.
32 devices in a mesh: seq: 8 (over z, x), wa: 4 (over y, core).
Axes of the slice: x: 2, y: 2, z: 4, core: 2. Of those that a mesh axis runs over, the one named last changes fastest.
Arguments:
- tokens: bfloat16 [8, 1024, 2048], P('wa', 'seq'), may hold values from -6 to 6
- lengths: int32 [8], P('wa'), may hold values from 256 to 1024, as said below
- norm_gain: float32 [2048], replicated, may hold values from 0.25 to 1.75
- in_weight: bfloat16 [2048, 8512], P('wa'), may hold values from -0.125 to 0.125
- conv_weight: float32 [4, 4352], replicated, may hold values from -3 to 3
- conv_bias: float32 [4352], replicated, may hold values from -1.8 to 1.8
- dt_bias: float32 [64], replicated, may hold values from -8 to -2
- a_log: float32 [64], replicated, may hold values from 0 to 2.77
- skip_gain: float32 [64], replicated, may hold values from 0.5 to 2
- out_gain: float32 [4096], replicated, may hold values from 0.25 to 1.75
- out_weight: bfloat16 [4096, 2048], P('wa'), may hold values from -0.09375 to 0.09375
- cotangent: bfloat16 [8, 1024, 2048], P('wa', 'seq'), may hold values from -6 to 6
Outputs:
- mixed_out: bfloat16 [8, 1024, 2048], P('wa', 'seq')
- grad_tokens: float32 [8, 1024, 2048], P('wa', 'seq')
- grad_norm_gain: float32 [2048], replicated
- grad_in_weight: float32 [2048, 8512], P('wa')
- grad_conv_weight: float32 [4, 4352], replicated
- grad_conv_bias: float32 [4352], replicated
- grad_dt_bias: float32 [64], replicated
- grad_a_log: float32 [64], replicated
- grad_skip: float32 [64], replicated
- grad_out_gain: float32 [4096], replicated
- grad_out_weight: float32 [4096, 2048], P('wa')
Inputs may be any that keep to these rules, and one draw needn't show every extreme that they name: `lengths`: each sequence's used slots come first; in each group of 2 sequences laid out on one index of wa one sequence is full.
All inputs are finite; a program needn't handle non-finite values.
Results may differ from a plain program's by a relative error of at most 0.012.
Values may be sent and summed in bfloat16 or wider, within the bound.
A program may use at most 384 MiB of HBM per device.

v0:
```python
import jax
import jax.numpy as jnp
from jax import lax
from jax.sharding import PartitionSpec as P

KW = 4
BLOCK_LEN = 256
EPS = 1e-05
HIGH = lax.Precision.HIGHEST


def row_scale(values):
    return lax.rsqrt(jnp.mean(values * values, axis=-1, keepdims=True) + EPS)


def norm_backward(values, row_scales, gain_vec, grad_out):
    weighted = grad_out * gain_vec
    grad_gain = jnp.sum(grad_out * values * row_scales, axis=0)
    grad_values = row_scales * weighted - values * row_scales**3 * jnp.mean(
        weighted * values, axis=-1, keepdims=True
    )
    return (grad_values, grad_gain)


def block_chain(x_heads, dt_vals, rates, b_rows, c_rows, block_len):
    seqs_here, length, head_total, head_size = x_heads.shape
    block_count = length // block_len
    states_dim = b_rows.shape[-1]
    x_blocks = x_heads.reshape(seqs_here, block_count, block_len, head_total, head_size)
    dt_blocks = jnp.swapaxes(dt_vals.reshape(seqs_here, block_count, block_len, head_total), 2, 3)
    rate_blocks = jnp.swapaxes(rates.reshape(seqs_here, block_count, block_len, head_total), 2, 3)
    b_blocks = b_rows.reshape(seqs_here, block_count, block_len, states_dim)
    c_blocks = c_rows.reshape(seqs_here, block_count, block_len, states_dim)
    cumulative = jnp.cumsum(rate_blocks, axis=-1)
    causal_mask = jnp.arange(block_len)[:, None] >= jnp.arange(block_len)[None, :]
    log_decay = cumulative[..., :, None] - cumulative[..., None, :]
    decay_matrix = jnp.where(causal_mask, jnp.exp(jnp.where(causal_mask, log_decay, 0.0)), 0.0)
    scores = jnp.einsum("sbin,sbjn->sbij", c_blocks, b_blocks, precision=HIGH)
    weights = scores[:, :, None] * decay_matrix * dt_blocks[..., None, :]
    inner_part = jnp.einsum("sbhij,sbjhp->sbihp", weights, x_blocks, precision=HIGH)
    tail_decay = jnp.exp(cumulative[..., -1:] - cumulative) * dt_blocks
    block_states = jnp.einsum(
        "sbhj,sbjhp,sbjn->sbhpn", tail_decay, x_blocks, b_blocks, precision=HIGH
    )
    block_decay = jnp.exp(cumulative[..., -1])

    def carry_step(carry_state, pieces):
        decay_now, state_now = pieces
        return (decay_now[..., None, None] * carry_state + state_now, carry_state)

    start_state = jnp.zeros((seqs_here, head_total, head_size, states_dim), jnp.float32)
    final_state, entering = lax.scan(
        carry_step, start_state, (jnp.moveaxis(block_decay, 1, 0), jnp.moveaxis(block_states, 1, 0))
    )
    entering = jnp.moveaxis(entering, 0, 1)
    carried = jnp.swapaxes(jnp.exp(cumulative), 2, 3)[..., None] * jnp.einsum(
        "sbin,sbhpn->sbihp", c_blocks, entering, precision=HIGH
    )
    output = (inner_part + carried).reshape(seqs_here, length, head_total, head_size)
    return (output, final_state)


def mixer_front(
    extended, dt_raw, conv_w, conv_b, bias_part, log_rates, x_width, state_size, head_size
):
    seqs_here = extended.shape[0]
    length = extended.shape[1] - (KW - 1)
    conv_sum = conv_b
    for offset in range(KW):
        conv_sum = conv_sum + conv_w[offset] * extended[:, offset : offset + length]
    activated = jax.nn.silu(conv_sum)
    x_heads = activated[..., :x_width].reshape(seqs_here, length, x_width // head_size, head_size)
    b_rows = activated[..., x_width : x_width + state_size]
    c_rows = activated[..., x_width + state_size :]
    dt_vals = jax.nn.softplus(dt_raw + bias_part)
    rates = -jnp.exp(log_rates) * dt_vals
    block_len = min(BLOCK_LEN, length)
    y_local, local_state = block_chain(x_heads, dt_vals, rates, b_rows, c_rows, block_len)
    running = jnp.exp(jnp.cumsum(rates, axis=1))
    total_decay = running[:, -1]
    return (y_local, local_state, total_decay, x_heads, c_rows, running)


def mixer_finish(y_local, x_heads, gate_part, skip_part):
    y_heads = y_local + skip_part[:, None] * x_heads
    seqs_here, length = (y_heads.shape[0], y_heads.shape[1])
    return y_heads.reshape(seqs_here, length, -1) * jax.nn.silu(gate_part)


def body(
    tokens,
    lengths,
    norm_gain,
    in_weight,
    conv_weight,
    conv_bias,
    dt_bias,
    a_log,
    skip_gain,
    out_gain,
    out_weight,
    cotangent,
):
    seqs_here, slot_rows, width = tokens.shape
    row_count = seqs_here * slot_rows
    inner_width = out_gain.shape[0]
    channels = conv_bias.shape[0]
    state_size = (channels - inner_width) // 2
    head_count = dt_bias.shape[0]
    head_size = inner_width // head_count
    seq_devices = lax.axis_size("seq")
    seq_index = lax.axis_index("seq")
    positions = seq_index * slot_rows + jnp.arange(slot_rows)
    valid_rows = (positions[None, :] < lengths[:, None]).astype(jnp.float32).reshape(row_count, 1)
    flat_tokens = tokens.reshape(row_count, width).astype(jnp.float32)
    in_scale = row_scale(flat_tokens)
    normed = (flat_tokens * in_scale * norm_gain).astype(jnp.bfloat16)
    columns = normed
    projected = jnp.dot(
        columns,
        lax.all_gather(in_weight, "wa", axis=0, tiled=True),
        preferred_element_type=jnp.float32,
    ).astype(jnp.bfloat16)
    gate_part = projected[:, :inner_width].reshape(seqs_here, slot_rows, inner_width)
    conv_in = projected[:, inner_width : inner_width + channels].reshape(
        seqs_here, slot_rows, channels
    )
    dt_raw = projected[:, inner_width + channels :].reshape(seqs_here, slot_rows, head_count)
    local_heads = head_count // seq_devices
    local_width = local_heads * head_size
    channel_start = seq_index * local_width
    head_start = seq_index * local_heads
    gate_heads, x_heads_in, dt_heads = (
        lax.all_to_all(gate_part, "seq", split_axis=2, concat_axis=1, tiled=True),
        lax.all_to_all(conv_in[..., :inner_width], "seq", split_axis=2, concat_axis=1, tiled=True),
        lax.all_to_all(dt_raw, "seq", split_axis=2, concat_axis=1, tiled=True),
    )
    bc_heads = lax.all_gather(conv_in[..., inner_width:], "seq", axis=1, tiled=True)
    joined = jnp.concatenate([x_heads_in, bc_heads], axis=2).astype(jnp.float32)
    extended = jnp.concatenate(
        [jnp.zeros((seqs_here, KW - 1, joined.shape[2]), jnp.float32), joined], axis=1
    )
    conv_local = jnp.concatenate(
        [
            lax.dynamic_slice_in_dim(conv_weight, channel_start, local_width, 1),
            conv_weight[:, inner_width:],
        ],
        axis=1,
    )
    bias_local = jnp.concatenate(
        [
            lax.dynamic_slice_in_dim(conv_bias, channel_start, local_width, 0),
            conv_bias[inner_width:],
        ],
        axis=0,
    )
    shift_local = lax.dynamic_slice_in_dim(dt_bias, head_start, local_heads, 0)
    rates_local = lax.dynamic_slice_in_dim(a_log, head_start, local_heads, 0)
    skip_local = lax.dynamic_slice_in_dim(skip_gain, head_start, local_heads, 0)

    def front_fn(extended_in, dt_in, conv_w, conv_b, bias_part, log_rates):
        return mixer_front(
            extended_in,
            dt_in,
            conv_w,
            conv_b,
            bias_part,
            log_rates,
            local_width,
            state_size,
            head_size,
        )

    front_out, front_pull = jax.vjp(
        front_fn,
        extended,
        dt_heads.astype(jnp.float32),
        conv_local,
        bias_local,
        shift_local,
        rates_local,
    )
    y_local, local_state, total_decay, x_heads, c_rows, running = front_out

    def finish_fn(y_in, x_in, gate_in, skip_in):
        return mixer_finish(y_in, x_in, gate_in, skip_in)

    gated_heads, finish_pull = jax.vjp(
        finish_fn, y_local, x_heads, gate_heads.astype(jnp.float32), skip_local
    )
    gated_tok = lax.all_to_all(
        gated_heads.astype(jnp.bfloat16), "seq", split_axis=1, concat_axis=2, tiled=True
    )
    gated_rows = gated_tok.reshape(row_count, inner_width).astype(jnp.float32)
    out_scale = row_scale(gated_rows)
    normed_out = (gated_rows * out_scale * out_gain).astype(jnp.bfloat16)
    columns = normed_out
    branch = jnp.dot(
        columns,
        lax.all_gather(out_weight, "wa", axis=0, tiled=True),
        preferred_element_type=jnp.float32,
    )
    mixed_out = (flat_tokens + valid_rows * branch).astype(jnp.bfloat16).reshape(tokens.shape)
    cot_rows = cotangent.reshape(row_count, width)
    branch_grad = cot_rows * valid_rows.astype(jnp.bfloat16)
    columns = normed_out
    out_weight_grad = lax.psum_scatter(
        lax.dot_general(
            columns, branch_grad, (((0,), (0,)), ((), ())), preferred_element_type=jnp.float32
        ),
        "wa",
        scatter_dimension=0,
        tiled=True,
    )
    normed_out_grad = lax.dot_general(
        branch_grad,
        lax.all_gather(out_weight, "wa", axis=0, tiled=True),
        (((1,), (1,)), ((), ())),
        preferred_element_type=jnp.float32,
    )
    gated_grad, out_gain_grad = norm_backward(gated_rows, out_scale, out_gain, normed_out_grad)
    gated_grad = gated_grad.astype(jnp.bfloat16).reshape(seqs_here, slot_rows, inner_width)
    grad_heads = lax.all_to_all(gated_grad, "seq", split_axis=2, concat_axis=1, tiled=True).astype(
        jnp.float32
    )
    y_grad, x_grad, gate_grad, skip_part_grad = finish_pull(grad_heads)
    front_grads = front_pull(
        (
            y_grad,
            jnp.zeros_like(local_state),
            jnp.zeros_like(total_decay),
            x_grad,
            jnp.zeros_like(c_rows),
            jnp.zeros_like(running),
        )
    )
    extended_grad, dt_grad, conv_w_grad, conv_b_grad, shift_grad, rates_grad = front_grads
    conv_heads_grad = extended_grad[:, KW - 1 :]
    gate_back, x_back, dt_back = (
        lax.all_to_all(
            gate_grad.astype(jnp.bfloat16), "seq", split_axis=1, concat_axis=2, tiled=True
        ),
        lax.all_to_all(
            conv_heads_grad[..., :local_width].astype(jnp.bfloat16),
            "seq",
            split_axis=1,
            concat_axis=2,
            tiled=True,
        ),
        lax.all_to_all(
            dt_grad.astype(jnp.bfloat16), "seq", split_axis=1, concat_axis=2, tiled=True
        ),
    )
    bc_back = lax.psum_scatter(
        conv_heads_grad[..., local_width:].astype(jnp.bfloat16),
        "seq",
        scatter_dimension=1,
        tiled=True,
    )
    proj_grad = jnp.concatenate([gate_back, x_back, bc_back, dt_back], axis=2)
    x_taps = lax.dynamic_update_slice_in_dim(
        jnp.zeros((KW, inner_width), jnp.float32), conv_w_grad[:, :local_width], channel_start, 1
    )
    conv_weight_grad = jnp.concatenate([x_taps, conv_w_grad[:, local_width:]], axis=1)
    x_bias = lax.dynamic_update_slice_in_dim(
        jnp.zeros((inner_width,), jnp.float32), conv_b_grad[:local_width], channel_start, 0
    )
    conv_bias_grad = jnp.concatenate([x_bias, conv_b_grad[local_width:]], axis=0)
    head_zeros = jnp.zeros((head_count,), jnp.float32)
    dt_bias_grad = lax.dynamic_update_slice_in_dim(head_zeros, shift_grad, head_start, 0)
    a_log_grad = lax.dynamic_update_slice_in_dim(head_zeros, rates_grad, head_start, 0)
    skip_grad = lax.dynamic_update_slice_in_dim(head_zeros, skip_part_grad, head_start, 0)
    proj_rows = proj_grad.reshape(row_count, proj_grad.shape[2])
    columns = normed
    in_weight_grad = lax.psum_scatter(
        lax.dot_general(
            columns, proj_rows, (((0,), (0,)), ((), ())), preferred_element_type=jnp.float32
        ),
        "wa",
        scatter_dimension=0,
        tiled=True,
    )
    normed_grad = lax.dot_general(
        proj_rows,
        lax.all_gather(in_weight, "wa", axis=0, tiled=True),
        (((1,), (1,)), ((), ())),
        preferred_element_type=jnp.float32,
    )
    token_grad, norm_gain_grad = norm_backward(flat_tokens, in_scale, norm_gain, normed_grad)
    token_grad = token_grad + cot_rows.astype(jnp.float32)
    in_weight_grad, out_weight_grad = lax.psum((in_weight_grad, out_weight_grad), "seq")
    small_grads = lax.psum(
        (
            norm_gain_grad,
            conv_weight_grad,
            conv_bias_grad,
            dt_bias_grad,
            a_log_grad,
            skip_grad,
            out_gain_grad,
        ),
        ("seq", "wa"),
    )
    return (
        mixed_out,
        token_grad.reshape(tokens.shape),
        small_grads[0],
        in_weight_grad,
        small_grads[1],
        small_grads[2],
        small_grads[3],
        small_grads[4],
        small_grads[5],
        small_grads[6],
        out_weight_grad,
    )


def solution(mesh):
    placed = (
        P("wa", "seq", None),
        P("wa"),
        P(),
        P("wa", None),
        P(),
        P(),
        P(),
        P(),
        P(),
        P(),
        P("wa", None),
        P("wa", "seq", None),
    )
    return jax.shard_map(
        body,
        mesh=mesh,
        in_specs=placed,
        out_specs=(
            P("wa", "seq", None),
            P("wa", "seq", None),
            P(),
            P("wa", None),
            P(),
            P(),
            P(),
            P(),
            P(),
            P(),
            P("wa", None),
        ),
        check_vma=False,
    )
```

profile of v0, /device:TPU:0, one launch (start us, length us, event | category | flops | bytes accessed | tf_op | source)
XLA Modules:
  0.0 2436.3 jit_solution(2501192697912139225)
XLA Ops:
  10.1 213.5 %all-gather.4.cloned.1.call-done = bf16[2048,8512]{0,1:T(8,128)(2,1)} async-done(((bf16[512,8512]{0,1:T(8,128)(2,1)}), bf16[2048,8512]{0,1:T(8,128)(2,1)}) %all-gather.4.cloned.1.call-update) | async-done | bytes 34865168 | tf_op jit(solution)/shard_map/all_gather | solution.py:121
  223.6 15.1 convolution_convert_fusion
  277.8 43.5 %all-to-all-done = bf16[2,128,4096]{1,0,2:T(2,128)(2,1)S(1)} async-done(((bf16[2,128,4096]{1,0,2:T(2,128)(2,1)}), bf16[2,128,4096]{1,0,2:T(2,128)(2,1)S(1)}, u32[]{:S(2)}, u32[]{:S(2)}) %all-to-all-start) | async-done | bytes 2097184 | tf_op jit(solution)/shard_map/all_to_all | solution.py:135
  376.8 19.7 bitcast_add_fusion.3
  433.1 43.9 %all-to-all-done.3 = bf16[2,1024,512]{2,0,1:T(2,128)(2,1)} async-done(((bf16[2,1024,512]{2,0,1:T(2,128)(2,1)}), bf16[2,1024,512]{2,0,1:T(2,128)(2,1)}, u32[]{:S(2)}, u32[]{:S(2)}) %all-to-all-start.3) | async-done | bytes 2097184 | tf_op jit(solution)/shard_map/all_to_all | solution.py:191
  495.5 14.9 multiply_reduce_fusion.7
  540.0 35.0 %all-to-all-done.4 = bf16[2,128,4096]{1,0,2:T(2,128)(2,1)} async-done(((bf16[2,128,4096]{1,0,2:T(2,128)(2,1)}), bf16[2,128,4096]{1,0,2:T(2,128)(2,1)}, u32[]{:S(2)}, u32[]{:S(2)}) %all-to-all-start.4) | async-done | bytes 2097184 | tf_op jit(solution)/shard_map/all_to_all | solution.py:223
  596.0 29.8 %fusion.9 = (f32[2,4,8,256]{3,2,1,0:T(8,128)S(1)}, f32[2,4,8,256]{3,2,1,0:T(8,128)S(1)}, f32[2,4,8,256]{3,2,1,0:T(8,128)}, f32[2,4,256,256]{3,2,1,0:T(8,128)}) fusion(f32[2,4,8,256]{3,2,1,0:T(8,128)S(1)} %get-tuple-element.439, f32[2,4,8,256]{3,2,1,0:T(8,128)S(1)} %get-tuple-element.437, f32[2,4,256,256]{3,2,1,0:T(8,128)S(1)} %copy-done.32, ...), kind=kOutput, calls=%fused_computation.21 | convolution fusion | flops 3283566592 | bytes 12976128 | tf_op jit(solution)/shard_map/transpose(jvp(sbhij,sbjhp->sbihp))/dot_general | solution.py:40
  664.3 15.5 bitcast_add_fusion.2
  751.6 13.3 fusion.136
  771.0 19.8 reduce-window.34
  792.0 19.8 reduce-window.36
  817.8 16.8 add_convert_fusion
  853.6 44.1 %all-to-all-done.6 = bf16[2,1024,512]{2,0,1:T(2,128)(2,1)} async-done(((bf16[2,1024,512]{2,0,1:T(2,128)(2,1)}), bf16[2,1024,512]{2,0,1:T(2,128)(2,1)}, u32[]{:S(2)}, u32[]{:S(2)}) %all-to-all-start.6) | async-done | bytes 2097184 | tf_op jit(solution)/shard_map/all_to_all | solution.py:243
  907.8 42.0 %all-to-all-done.5 = bf16[2,1024,512]{2,0,1:T(2,128)(2,1)} async-done(((bf16[2,1024,512]{2,0,1:T(2,128)(2,1)}), bf16[2,1024,512]{2,0,1:T(2,128)(2,1)}, u32[]{:S(2)}, u32[]{:S(2)}) %all-to-all-start.5) | async-done | bytes 2097184 | tf_op jit(solution)/shard_map/all_to_all | solution.py:240
  954.8 28.3 %fusion.95 = f32[2048,8512]{0,1:T(8,128)} fusion(bf16[256,2048]{1,0:T(8,128)(2,1)} %copy-done.29, bf16[256,64]{1,0:T(8,128)(2,1)S(1)} %copy.528, bf16[256,256]{1,0:T(8,128)(2,1)S(1)} %bitcast.400, bf16[256,4096]{1,0:T(8,128)(2,1)S(1)} %bitcast.377, bf16[256,4096]{1,0:T(8,128)(2,1)} %bitcast.379), kind=kOutput, calls=%fused_computation.140 | convolution fusion | flops 8942911488 | bytes 75137024 | tf_op jit(solution)/shard_map/dot_general | solution.py:276
  984.6 59.7 %reduce-scatter.8.cloned.1.call-done = f32[1024,2048]{1,0:T(8,128)} async-done(((f32[4096,2048]{1,0:T(8,128)}), f32[1024,2048]{1,0:T(8,128)}) %reduce-scatter.8.cloned.1.call-update) | async-done | bytes 8388624 | tf_op jit(solution)/shard_map/reduce_scatter | solution.py:207
  1044.3 471.0 %reduce-scatter.6.cloned.1.call-done = f32[512,8512]{0,1:T(8,128)} async-done(((f32[2048,8512]{0,1:T(8,128)}), f32[512,8512]{0,1:T(8,128)}) %reduce-scatter.6.cloned.1.call-update) | async-done | bytes 17432592 | tf_op jit(solution)/shard_map/reduce_scatter | solution.py:275
  1516.6 12.6 fusion.49
  1530.5 18.1 fusion.58
  1548.7 40.5 %all-reduce.14 = (f32[2048]{0:T(1024)}, f32[4352]{0:T(1024)}, f32[64]{0:T(128)}, f32[64]{0:T(128)}, f32[64]{0:T(128)}, /*index=5*/f32[4096]{0:T(1024)}) all-reduce(f32[2048]{0:T(1024)S(1)} %get-tuple-element.389, f32[4352]{0:T(1024)S(1)} %pad_maximum_fusion.4, ...), channel_id=1, replica_groups=mesh['seq'=8,'wa'=4] {'seq','wa'}, use_global_device_ids=true, to_apply=%region_25.26 | all-reduce | flops 10688 | bytes 85504 | tf_op jit(solution)/shard_map/psum | solution.py:292
  1592.8 46.6 %all-reduce.19.cloned.1.call-done = f32[4,4352]{1,0:T(4,128)} async-done(((f32[4,4352]{1,0:T(4,128)}), f32[4,4352]{1,0:T(4,128)}) %all-reduce.19.cloned.1.call-update) | async-done | bytes 69648 | tf_op jit(solution)/shard_map/psum | solution.py:292
  1639.4 772.4 %all-reduce.21.cloned.1.call-done = (f32[512,8512]{0,1:T(8,128)}, f32[1024,2048]{1,0:T(8,128)}) async-done(((f32[512,8512]{0,1:T(8,128)}, f32[1024,2048]{1,0:T(8,128)}), (f32[512,8512]{0,1:T(8,128)}, f32[1024,2048]{1,0:T(8,128)})) %all-reduce.21.cloned.1.call-update) | async-done | bytes 25821200 | tf_op jit(solution)/shard_map/psum | solution.py:291
  2411.8 13.4 copy.711
  (405 shorter events, 384.7 us)
Async XLA Ops:
  7.2 216.4 %all-gather.4.cloned.1.call-start = ((), (), s32[]{:S(2)}) async-start(), calls=%async_computation.11 | async-start | bytes 43581440 | tf_op jit(solution)/shard_map/all_gather | solution.py:121
  7.9 323.9 %all-gather.6.cloned.1.call-start = ((), (), s32[]{:S(2)}) async-start(), calls=%async_computation.12 | async-start | bytes 1179648 | tf_op jit(solution)/shard_map/all_gather | solution.py:138
  10.1 228.5 %copy-start.29 = (bf16[256,2048]{1,0:T(8,128)(2,1)}, bf16[256,2048]{1,0:T(8,128)(2,1)S(1)}, u32[]{:S(2)}) copy-start(bf16[256,2048]{1,0:T(8,128)(2,1)S(1)} %fusion.52) | copy-start | bytes 3145732
  247.5 248.0 %all-gather.8.cloned.1.call-start = ((), (), s32[]{:S(2)}) async-start(), calls=%async_computation.13 | async-start | bytes 20971520 | tf_op jit(solution)/shard_map/all_gather | solution.py:200
  248.9 12.2 all-to-all-start.1
  261.1 60.2 %all-to-all-start = ((bf16[2,128,4096]{1,0,2:T(2,128)(2,1)}), bf16[2,128,4096]{1,0,2:T(2,128)(2,1)S(1)}, u32[]{:S(2)}, u32[]{:S(2)}) async-start(bf16[2,128,4096]{1,0,2:T(2,128)(2,1)} %slice.142), calls=%async_computation | async-start | bytes 4194304 | tf_op jit(solution)/shard_map/all_to_all | solution.py:135
  265.1 146.7 %copy-start.52 = (f32[512]{0:T(512)}, f32[512]{0:T(512)S(1)}, u32[]{:S(2)}) copy-start(f32[512]{0:T(512)S(1)} %mul.518) | copy-start | bytes 6148
  265.2 69.3 %copy-start.41 = (f32[768]{0:T(1024)}, f32[768]{0:T(1024)S(1)}, u32[]{:S(2)}) copy-start(f32[768]{0:T(1024)S(1)} %get-tuple-element.391) | copy-start | bytes 9220
  265.2 69.3 %copy-start.43 = (f32[768]{0:T(1024)}, f32[768]{0:T(1024)S(1)}, u32[]{:S(2)}) copy-start(f32[768]{0:T(1024)S(1)} %get-tuple-element.392) | copy-start | bytes 9220
  265.2 69.3 %copy-start.45 = (f32[768]{0:T(1024)}, f32[768]{0:T(1024)S(1)}, u32[]{:S(2)}) copy-start(f32[768]{0:T(1024)S(1)} %get-tuple-element.393) | copy-start | bytes 9220
  265.2 69.3 %copy-start.47 = (f32[768]{0:T(1024)}, f32[768]{0:T(1024)S(1)}, u32[]{:S(2)}) copy-start(f32[768]{0:T(1024)S(1)} %get-tuple-element.394) | copy-start | bytes 9220
  277.6 50.9 %copy-start.36 = (f32[2,4,8]{2,1,0:T(4,128)}, f32[2,4,8]{2,1,0:T(4,128)S(1)}, u32[]{:S(2)}) copy-start(f32[2,4,8]{2,1,0:T(4,128)S(1)} %slice_reduce_fusion.2) | copy-start | bytes 772
  321.3 85.9 %all-to-all-start.2 = ((bf16[2,128,4096]{1,0,2:T(2,128)(2,1)}), bf16[2,128,4096]{1,0,2:T(2,128)(2,1)}, u32[]{:S(2)}, u32[]{:S(2)}) async-start(bf16[2,128,4096]{1,0,2:T(2,128)(2,1)} %reshape.388), calls=%async_computation.2 | async-start | bytes 4194304 | tf_op jit(solution)/shard_map/all_to_all | solution.py:134
  424.1 53.0 %all-to-all-start.3 = ((bf16[2,1024,512]{2,0,1:T(2,128)(2,1)}), bf16[2,1024,512]{2,0,1:T(2,128)(2,1)}, u32[]{:S(2)}, u32[]{:S(2)}) async-start(bf16[2,1024,512]{2,0,1:T(2,128)(2,1)} %copy.495), calls=%async_computation.3 | async-start | bytes 4194304 | tf_op jit(solution)/shard_map/all_to_all | solution.py:191
  522.8 52.2 %all-to-all-start.4 = ((bf16[2,128,4096]{1,0,2:T(2,128)(2,1)}), bf16[2,128,4096]{1,0,2:T(2,128)(2,1)}, u32[]{:S(2)}, u32[]{:S(2)}) async-start(bf16[2,128,4096]{1,0,2:T(2,128)(2,1)} %copy.498), calls=%async_computation.4 | async-start | bytes 4194304 | tf_op jit(solution)/shard_map/all_to_all | solution.py:223
  527.2 376.0 %reduce-scatter.10.cloned.1.call-start = ((), (), s32[]{:S(2)}) async-start(), calls=%async_computation.17 | async-start | bytes 1179648
  745.3 299.0 %reduce-scatter.8.cloned.1.call-start = ((), (), s32[]{:S(2)}) async-start(), calls=%async_computation.16 | async-start | bytes 41943040 | tf_op jit(solution)/shard_map/reduce_scatter | solution.py:207
  814.0 29.6 %all-to-all-start.7 = ((bf16[8,2,1024]{2,1,0:T(2,128)(2,1)}), bf16[8,2,1024]{2,1,0:T(2,128)(2,1)S(1)}, u32[]{:S(2)}, u32[]{:S(2)}) async-start(bf16[8,2,1024]{2,1,0:T(2,128)(2,1)} %reshape.438), calls=%async_computation.7 | async-start | bytes 65536 | tf_op jit(solution)/shard_map/all_to_all | solution.py:250
  843.6 54.1 %all-to-all-start.6 = ((bf16[2,1024,512]{2,0,1:T(2,128)(2,1)}), bf16[2,1024,512]{2,0,1:T(2,128)(2,1)}, u32[]{:S(2)}, u32[]{:S(2)}) async-start(bf16[2,1024,512]{2,0,1:T(2,128)(2,1)} %copy.517), calls=%async_computation.6 | async-start | bytes 4194304 | tf_op jit(solution)/shard_map/all_to_all | solution.py:243
  897.7 52.2 %all-to-all-start.5 = ((bf16[2,1024,512]{2,0,1:T(2,128)(2,1)}), bf16[2,1024,512]{2,0,1:T(2,128)(2,1)}, u32[]{:S(2)}, u32[]{:S(2)}) async-start(bf16[2,1024,512]{2,0,1:T(2,128)(2,1)} %copy.501), calls=%async_computation.5 | async-start | bytes 4194304 | tf_op jit(solution)/shard_map/all_to_all | solution.py:240
  902.0 613.3 %reduce-scatter.6.cloned.1.call-start = ((), (), s32[]{:S(2)}) async-start(), calls=%async_computation.14 | async-start | bytes 87162880 | tf_op jit(solution)/shard_map/reduce_scatter | solution.py:275
  907.8 47.0 %copy-start.26 = (bf16[32,8,8,512]{3,1,2,0:T(8,128)(2,1)}, bf16[32,8,8,512]{3,1,2,0:T(8,128)(2,1)S(1)}, u32[]{:S(2)}) copy-start(bf16[32,8,8,512]{3,1,2,0:T(8,128)(2,1)S(1)} %copy.597) | copy-start | bytes 6291460
  983.1 656.3 %all-reduce.19.cloned.1.call-start = ((), (), s32[]{:S(2)}) async-start(), calls=%async_computation.15 | async-start | bytes 139264 | tf_op jit(solution)/shard_map/psum | solution.py:292
  984.6 1427.2 %all-reduce.21.cloned.1.call-start = ((), (), s32[]{:S(2)}) async-start(), calls=%async_computation.18 | async-start | bytes 51642368 | tf_op jit(solution)/shard_map/psum | solution.py:291
  (80 other events, 705.0 us)
Sparse Core Ops, SparseCore 0:
  9.6 213.9 all-gather.3
  247.6 67.1 all-gather.5
  316.4 104.4 all-gather.7
  745.5 62.2 reduce-scatter.9
  810.4 233.8 reduce-scatter.7
  1047.0 468.2 reduce-scatter.5
  1521.5 117.8 all-reduce.18
  1643.8 767.9 all-reduce.20
where the time goes:
time: 2440 us
  waiting for transfers between devices  1780 us (73%)
  matrix products  219 us (9%)
  local copies, waits for them, and re-layouts  179 us (7%)
  other arithmetic  166 us (7%)
  blocking collectives  40.5 us (2%)
  starting transfers between devices  38.5 us (2%)
    psum x1, waiting for transfers between devices, body(): lax.psum((in_weight_grad, out_weight_grad), 'seq')  772 us
    reduce_scatter x1, waiting for transfers between devices, body(): lax.psum_scatter(lax.dot_general(columns, proj_rows, (((0,), (0,)), ((),...  471 us
    all_gather x1, waiting for transfers between devices, body(): lax.all_gather(in_weight, 'wa', axis=0, tiled=True)  213 us
    another operation x14, other arithmetic  71.1 us
    dot_general x3, matrix products, block_chain(): jnp.einsum('sbhij,sbjhp->sbihp', weights, x_blocks, precision=HIGH)  65 us
    reduce_scatter x1, waiting for transfers between devices, body(): lax.psum_scatter(lax.dot_general(columns, branch_grad, (((0,), (0,)), (()...  59.7 us
    unnamed x184, local copies, waits for them, and re-layouts  53.7 us
  transfers between devices with their start and end apart: 16, of which 11 were waited for; matrix products, arithmetic and copies ran while one was open for 13% of the time, Pallas kernels for 0%

commit v1 on v0

--- a/solution.py
+++ b/solution.py
@@ -289,18 +289,17 @@
     token_grad, norm_gain_grad = norm_backward(flat_tokens, in_scale, norm_gain, normed_grad)
     token_grad = token_grad + cot_rows.astype(jnp.float32)
     in_weight_grad, out_weight_grad = lax.psum((in_weight_grad, out_weight_grad), "seq")
-    small_grads = lax.psum(
-        (
-            norm_gain_grad,
-            conv_weight_grad,
-            conv_bias_grad,
-            dt_bias_grad,
-            a_log_grad,
-            skip_grad,
-            out_gain_grad,
-        ),
-        ("seq", "wa"),
-    )
+    small_grads = (
+        norm_gain_grad,
+        conv_weight_grad,
+        conv_bias_grad,
+        dt_bias_grad,
+        a_log_grad,
+        skip_grad,
+        out_gain_grad,
+    )
+    for axis in ("wa", "seq"):
+        small_grads = lax.psum(small_grads, axis)
     return (
         mixed_out,
         token_grad.reshape(tokens.shape),

time: 2440 us -> 2360 us (0.967)
  waiting for transfers between devices: 1780 us -> 1680 us
    psum x1, waiting for transfers between devices: 772 us -> 686 us  [body(): lax.psum((in_weight_grad, out_weight_grad), 'seq')]
    psum x1, waiting for transfers between devices: 46.6 us -> 0.02 us  [body(): small_grads = lax.psum(small_grads, axis)]
    reduce_scatter x1, waiting for transfers between devices: 59.7 us -> 98.3 us  [body(): lax.psum_scatter(lax.dot_general(columns, branch_grad, (((0,), (0,)), (()...]
    psum x1 -> x2, blocking collectives: 40.5 us -> 52.1 us  [body(): small_grads = lax.psum(small_grads, axis)]
    unnamed x184 -> x186, local copies, waits for them, and re-layouts: 53.7 us -> 53.1 us
  transfers between devices with their start and end apart: 16 -> 16, of which waited for: 11 -> 10; matrix products, arithmetic and copies ran while one was open for 13% -> 13% of each run, Pallas kernels for 0% -> 0%
where the time goes in v1:
time: 2360 us; the launch traced here: 2350 us
  waiting for transfers between devices  1680 us (71%)
  matrix products  220 us (9%)
  local copies, waits for them, and re-layouts  177 us (8%)
  other arithmetic  161 us (7%)
  blocking collectives  52.1 us (2%)
  starting transfers between devices  39.1 us (2%)
    psum x1, waiting for transfers between devices, body(): lax.psum((in_weight_grad, out_weight_grad), 'seq')  686 us
    reduce_scatter x1, waiting for transfers between devices, body(): lax.psum_scatter(lax.dot_general(columns, proj_rows, (((0,), (0,)), ((),...  471 us
    all_gather x1, waiting for transfers between devices, body(): lax.all_gather(in_weight, 'wa', axis=0, tiled=True)  213 us
    reduce_scatter x1, waiting for transfers between devices, body(): lax.psum_scatter(lax.dot_general(columns, branch_grad, (((0,), (0,)), (()...  98.3 us
    another operation x14, other arithmetic  65.4 us
    dot_general x3, matrix products, block_chain(): jnp.einsum('sbhij,sbjhp->sbihp', weights, x_blocks, precision=HIGH)  64.8 us
    unnamed x186, local copies, waits for them, and re-layouts  53.1 us
    psum x2, blocking collectives, body(): small_grads = lax.psum(small_grads, axis)  52.1 us
  transfers between devices with their start and end apart: 16, of which 10 were waited for; matrix products, arithmetic and copies ran while one was open for 13% of the time, Pallas kernels for 0%

profile of v1, /device:TPU:0, one launch (start us, length us, event | category | flops | bytes accessed | tf_op | source)
XLA Modules:
  0.0 2349.2 jit_solution(12366420811468137577)
XLA Ops:
  10.1 213.5 %all-gather.4.cloned.1.call-done = bf16[2048,8512]{0,1:T(8,128)(2,1)} async-done(((bf16[512,8512]{0,1:T(8,128)(2,1)}), bf16[2048,8512]{0,1:T(8,128)(2,1)}) %all-gather.4.cloned.1.call-update) | async-done | bytes 34865168 | tf_op jit(solution)/shard_map/all_gather | solution.py:121
  223.6 15.1 convolution_convert_fusion
  277.8 43.5 %all-to-all-done = bf16[2,128,4096]{1,0,2:T(2,128)(2,1)S(1)} async-done(((bf16[2,128,4096]{1,0,2:T(2,128)(2,1)}), bf16[2,128,4096]{1,0,2:T(2,128)(2,1)S(1)}, u32[]{:S(2)}, u32[]{:S(2)}) %all-to-all-start) | async-done | bytes 2097184 | tf_op jit(solution)/shard_map/all_to_all | solution.py:135
  376.8 19.7 bitcast_add_fusion.3
  433.1 44.0 %all-to-all-done.3 = bf16[2,1024,512]{2,0,1:T(2,128)(2,1)} async-done(((bf16[2,1024,512]{2,0,1:T(2,128)(2,1)}), bf16[2,1024,512]{2,0,1:T(2,128)(2,1)}, u32[]{:S(2)}, u32[]{:S(2)}) %all-to-all-start.3) | async-done | bytes 2097184 | tf_op jit(solution)/shard_map/all_to_all | solution.py:191
  495.6 15.1 multiply_reduce_fusion.7
  540.0 35.3 %all-to-all-done.4 = bf16[2,128,4096]{1,0,2:T(2,128)(2,1)} async-done(((bf16[2,128,4096]{1,0,2:T(2,128)(2,1)}), bf16[2,128,4096]{1,0,2:T(2,128)(2,1)}, u32[]{:S(2)}, u32[]{:S(2)}) %all-to-all-start.4) | async-done | bytes 2097184 | tf_op jit(solution)/shard_map/all_to_all | solution.py:223
  596.3 29.8 %fusion.9 = (f32[2,4,8,256]{3,2,1,0:T(8,128)S(1)}, f32[2,4,8,256]{3,2,1,0:T(8,128)S(1)}, f32[2,4,8,256]{3,2,1,0:T(8,128)}, f32[2,4,256,256]{3,2,1,0:T(8,128)}) fusion(f32[2,4,8,256]{3,2,1,0:T(8,128)S(1)} %get-tuple-element.446, f32[2,4,8,256]{3,2,1,0:T(8,128)S(1)} %get-tuple-element.444, f32[2,4,256,256]{3,2,1,0:T(8,128)S(1)} %copy-done.32, ...), kind=kOutput, calls=%fused_computation.21 | convolution fusion | flops 3283566592 | bytes 12976128 | tf_op jit(solution)/shard_map/transpose(jvp(sbhij,sbjhp->sbihp))/dot_general | solution.py:40
  664.8 15.3 bitcast_add_fusion.2
  753.9 14.6 fusion.136
  774.5 19.8 reduce-window.34
  795.5 19.8 reduce-window.36
  821.0 11.1 add_convert_fusion
  850.7 43.9 %all-to-all-done.6 = bf16[2,1024,512]{2,0,1:T(2,128)(2,1)} async-done(((bf16[2,1024,512]{2,0,1:T(2,128)(2,1)}), bf16[2,1024,512]{2,0,1:T(2,128)(2,1)}, u32[]{:S(2)}, u32[]{:S(2)}) %all-to-all-start.6) | async-done | bytes 2097184 | tf_op jit(solution)/shard_map/all_to_all | solution.py:243
  905.0 41.9 %all-to-all-done.5 = bf16[2,1024,512]{2,0,1:T(2,128)(2,1)} async-done(((bf16[2,1024,512]{2,0,1:T(2,128)(2,1)}), bf16[2,1024,512]{2,0,1:T(2,128)(2,1)}, u32[]{:S(2)}, u32[]{:S(2)}) %all-to-all-start.5) | async-done | bytes 2097184 | tf_op jit(solution)/shard_map/all_to_all | solution.py:240
  951.8 28.2 %fusion.95 = f32[2048,8512]{0,1:T(8,128)} fusion(bf16[256,2048]{1,0:T(8,128)(2,1)} %copy-done.29, bf16[256,64]{1,0:T(8,128)(2,1)S(1)} %copy.528, bf16[256,256]{1,0:T(8,128)(2,1)S(1)} %bitcast.400, bf16[256,4096]{1,0:T(8,128)(2,1)S(1)} %bitcast.377, bf16[256,4096]{1,0:T(8,128)(2,1)} %bitcast.379), kind=kOutput, calls=%fused_computation.140 | convolution fusion | flops 8942911488 | bytes 75137024 | tf_op jit(solution)/shard_map/dot_general | solution.py:276
  980.3 98.3 %reduce-scatter.8.cloned.1.call-done = f32[1024,2048]{1,0:T(8,128)} async-done(((f32[4096,2048]{1,0:T(8,128)}), f32[1024,2048]{1,0:T(8,128)}) %reduce-scatter.8.cloned.1.call-update) | async-done | bytes 8388624 | tf_op jit(solution)/shard_map/reduce_scatter | solution.py:207
  1078.6 470.9 %reduce-scatter.6.cloned.1.call-done = f32[512,8512]{0,1:T(8,128)} async-done(((f32[2048,8512]{0,1:T(8,128)}), f32[512,8512]{0,1:T(8,128)}) %reduce-scatter.6.cloned.1.call-update) | async-done | bytes 17432592 | tf_op jit(solution)/shard_map/reduce_scatter | solution.py:275
  1550.8 12.6 fusion.49
  1564.6 18.2 fusion.58
  1582.7 11.4 all-reduce.16
  1594.1 40.7 %all-reduce.14 = (f32[2048]{0:T(1024)}, f32[4352]{0:T(1024)}, f32[64]{0:T(128)}, f32[64]{0:T(128)}, f32[64]{0:T(128)}, /*index=5*/f32[4096]{0:T(1024)}) all-reduce(f32[2048]{0:T(1024)S(1)} %get-tuple-element.430, f32[4352]{0:T(1024)S(1)} %get-tuple-element.431, ...), channel_id=1, replica_groups=mesh['seq'=8,'wa'=4] {'seq'}, use_global_device_ids=true, to_apply=%region_26.27 | all-reduce | flops 10688 | bytes 85504 | tf_op jit(solution)/shard_map/psum | solution.py:302
  1638.4 686.3 %all-reduce.22.cloned.1.call-done = (f32[512,8512]{0,1:T(8,128)}, f32[4,4352]{1,0:T(4,128)}, f32[1024,2048]{1,0:T(8,128)}) async-done(((f32[512,8512]{0,1:T(8,128)}, f32[4,4352]{1,0:T(4,128)}, f32[1024,2048]{1,0:T(8,128)}), (f32[512,8512]{0,1:T(8,128)}, f32[4,4352]{1,0:T(4,128)}, f32[1024,2048]{1,0:T(8,128)})) %all-reduce.22.cloned.1.call-update) | async-done | bytes 25890832 | tf_op jit(solution)/shard_map/psum | solution.py:291
  2324.7 13.4 copy.712
  (408 shorter events, 384.8 us)
Async XLA Ops:
  7.2 216.4 %all-gather.4.cloned.1.call-start = ((), (), s32[]{:S(2)}) async-start(), calls=%async_computation.11 | async-start | bytes 43581440 | tf_op jit(solution)/shard_map/all_gather | solution.py:121
  7.9 324.1 %all-gather.6.cloned.1.call-start = ((), (), s32[]{:S(2)}) async-start(), calls=%async_computation.12 | async-start | bytes 1179648 | tf_op jit(solution)/shard_map/all_gather | solution.py:138
  10.1 228.5 %copy-start.29 = (bf16[256,2048]{1,0:T(8,128)(2,1)}, bf16[256,2048]{1,0:T(8,128)(2,1)S(1)}, u32[]{:S(2)}) copy-start(bf16[256,2048]{1,0:T(8,128)(2,1)S(1)} %fusion.52) | copy-start | bytes 3145732
  247.5 248.0 %all-gather.8.cloned.1.call-start = ((), (), s32[]{:S(2)}) async-start(), calls=%async_computation.13 | async-start | bytes 20971520 | tf_op jit(solution)/shard_map/all_gather | solution.py:200
  248.9 12.2 all-to-all-start.1
  261.1 60.2 %all-to-all-start = ((bf16[2,128,4096]{1,0,2:T(2,128)(2,1)}), bf16[2,128,4096]{1,0,2:T(2,128)(2,1)S(1)}, u32[]{:S(2)}, u32[]{:S(2)}) async-start(bf16[2,128,4096]{1,0,2:T(2,128)(2,1)} %slice.142), calls=%async_computation | async-start | bytes 4194304 | tf_op jit(solution)/shard_map/all_to_all | solution.py:135
  265.1 146.7 %copy-start.52 = (f32[512]{0:T(512)}, f32[512]{0:T(512)S(1)}, u32[]{:S(2)}) copy-start(f32[512]{0:T(512)S(1)} %mul.518) | copy-start | bytes 6148
  265.2 69.6 %copy-start.41 = (f32[768]{0:T(1024)}, f32[768]{0:T(1024)S(1)}, u32[]{:S(2)}) copy-start(f32[768]{0:T(1024)S(1)} %get-tuple-element.391) | copy-start | bytes 9220
  265.2 69.6 %copy-start.43 = (f32[768]{0:T(1024)}, f32[768]{0:T(1024)S(1)}, u32[]{:S(2)}) copy-start(f32[768]{0:T(1024)S(1)} %get-tuple-element.392) | copy-start | bytes 9220
  265.2 69.6 %copy-start.45 = (f32[768]{0:T(1024)}, f32[768]{0:T(1024)S(1)}, u32[]{:S(2)}) copy-start(f32[768]{0:T(1024)S(1)} %get-tuple-element.393) | copy-start | bytes 9220
  265.2 69.6 %copy-start.47 = (f32[768]{0:T(1024)}, f32[768]{0:T(1024)S(1)}, u32[]{:S(2)}) copy-start(f32[768]{0:T(1024)S(1)} %get-tuple-element.394) | copy-start | bytes 9220
  277.6 51.2 %copy-start.36 = (f32[2,4,8]{2,1,0:T(4,128)}, f32[2,4,8]{2,1,0:T(4,128)S(1)}, u32[]{:S(2)}) copy-start(f32[2,4,8]{2,1,0:T(4,128)S(1)} %slice_reduce_fusion.2) | copy-start | bytes 772
  321.3 85.8 %all-to-all-start.2 = ((bf16[2,128,4096]{1,0,2:T(2,128)(2,1)}), bf16[2,128,4096]{1,0,2:T(2,128)(2,1)}, u32[]{:S(2)}, u32[]{:S(2)}) async-start(bf16[2,128,4096]{1,0,2:T(2,128)(2,1)} %reshape.388), calls=%async_computation.2 | async-start | bytes 4194304 | tf_op jit(solution)/shard_map/all_to_all | solution.py:134
  424.1 53.0 %all-to-all-start.3 = ((bf16[2,1024,512]{2,0,1:T(2,128)(2,1)}), bf16[2,1024,512]{2,0,1:T(2,128)(2,1)}, u32[]{:S(2)}, u32[]{:S(2)}) async-start(bf16[2,1024,512]{2,0,1:T(2,128)(2,1)} %copy.495), calls=%async_computation.3 | async-start | bytes 4194304 | tf_op jit(solution)/shard_map/all_to_all | solution.py:191
  523.1 52.2 %all-to-all-start.4 = ((bf16[2,128,4096]{1,0,2:T(2,128)(2,1)}), bf16[2,128,4096]{1,0,2:T(2,128)(2,1)}, u32[]{:S(2)}, u32[]{:S(2)}) async-start(bf16[2,128,4096]{1,0,2:T(2,128)(2,1)} %copy.498), calls=%async_computation.4 | async-start | bytes 4194304 | tf_op jit(solution)/shard_map/all_to_all | solution.py:223
  527.4 372.9 %reduce-scatter.10.cloned.1.call-start = ((), (), s32[]{:S(2)}) async-start(), calls=%async_computation.17 | async-start | bytes 1179648
  745.7 234.7 %all-reduce.20.cloned.1.call-start = ((), (), s32[]{:S(2)}) async-start(), calls=%async_computation.15 | async-start | bytes 139264 | tf_op jit(solution)/shard_map/psum | solution.py:302
  753.8 324.8 %reduce-scatter.8.cloned.1.call-start = ((), (), s32[]{:S(2)}) async-start(), calls=%async_computation.16 | async-start | bytes 41943040 | tf_op jit(solution)/shard_map/reduce_scatter | solution.py:207
  817.4 23.3 all-to-all-start.7
  840.7 54.0 %all-to-all-start.6 = ((bf16[2,1024,512]{2,0,1:T(2,128)(2,1)}), bf16[2,1024,512]{2,0,1:T(2,128)(2,1)}, u32[]{:S(2)}, u32[]{:S(2)}) async-start(bf16[2,1024,512]{2,0,1:T(2,128)(2,1)} %copy.517), calls=%async_computation.6 | async-start | bytes 4194304 | tf_op jit(solution)/shard_map/all_to_all | solution.py:243
  894.7 52.2 %all-to-all-start.5 = ((bf16[2,1024,512]{2,0,1:T(2,128)(2,1)}), bf16[2,1024,512]{2,0,1:T(2,128)(2,1)}, u32[]{:S(2)}, u32[]{:S(2)}) async-start(bf16[2,1024,512]{2,0,1:T(2,128)(2,1)} %copy.501), calls=%async_computation.5 | async-start | bytes 4194304 | tf_op jit(solution)/shard_map/all_to_all | solution.py:240
  899.0 650.5 %reduce-scatter.6.cloned.1.call-start = ((), (), s32[]{:S(2)}) async-start(), calls=%async_computation.14 | async-start | bytes 87162880 | tf_op jit(solution)/shard_map/reduce_scatter | solution.py:275
  905.0 46.9 %copy-start.26 = (bf16[32,8,8,512]{3,1,2,0:T(8,128)(2,1)}, bf16[32,8,8,512]{3,1,2,0:T(8,128)(2,1)S(1)}, u32[]{:S(2)}) copy-start(bf16[32,8,8,512]{3,1,2,0:T(8,128)(2,1)S(1)} %copy.597) | copy-start | bytes 6291460
  980.1 1344.7 %all-reduce.22.cloned.1.call-start = ((), (), s32[]{:S(2)}) async-start(), calls=%async_computation.18 | async-start | bytes 51781632 | tf_op jit(solution)/shard_map/psum | solution.py:291
  (81 other events, 726.6 us)
Sparse Core Ops, SparseCore 0:
  9.6 213.9 all-gather.3
  247.6 67.1 all-gather.5
  316.4 104.4 all-gather.7
  745.8 62.4 reduce-scatter.9
  811.2 28.1 all-reduce.19
  841.8 236.7 reduce-scatter.7
  1081.3 468.2 reduce-scatter.5
  1555.2 769.5 all-reduce.21
